TPU v7x, 256 devices: a whole 4x4x8 slice. The times are simulated.
256 devices in a mesh: row: 8 (over x, core), col: 32 (over y, z).
Axes of the slice: x: 4, y: 4, z: 8, core: 2. Of those that a mesh axis runs over, the one named last changes fastest.
Arguments:
- factor: float32 [6, 8, 32, 512, 512], P(None, 'row', 'col'), may hold values from -0.1875 to 0.1875
- rhs: float32 [6, 8, 32, 128, 128], P(None, 'row', 'col'), may hold values from -6 to 6
- inverses: float32 [4, 512, 512], replicated, may hold values from -0.5 to 2, as said below
Outputs:
- solved: float32 [4, 512, 128], P(None, 'col')
- remaining: float32 [6, 8, 32, 128, 128], P(None, 'row', 'col')
Inputs may be any that keep to these rules, and one draw needn't show every extreme that they name: `inverses`: each block is lower triangular with its diagonal between 0.5 and 2 and entries below it of magnitude at most 4 / sqrt(512).
All inputs are finite; a program needn't handle non-finite values.
Results may differ from a plain program's by a relative error of at most 0.00011.
Values sent between devices are 32-bit elements; how exact they have to be, the bound alone decides.
A program may use at most 64 MiB of HBM per device.

v0:
```python
import jax
import jax.numpy as jnp
from jax import lax
from jax.sharding import PartitionSpec as P


def shifted(block, axis, distance):
    devices = range(lax.axis_size(axis))
    route = [((i - distance) % len(devices), i) for i in devices]
    return lax.ppermute(block, axis, route)


def broadcast(x, axis, root):
    mine = lax.axis_index(axis) == root
    return lax.psum(jnp.where(mine, x, jnp.zeros_like(x)), axis)


def group_reduce(update, member, steps, groups):
    blocks = update.shape[0]
    nrhs = update.shape[2]
    split = update.reshape(blocks, steps, update.shape[1] // steps, nrhs)
    total = lax.dynamic_index_in_dim(split, member, 1, keepdims=False)
    for offset in range(1, steps):
        piece = lax.dynamic_index_in_dim(split, (member + offset) % steps, 1, keepdims=False)
        total = total + shifted(piece, "col", offset * groups)
    return total


def on_device(factor, rhs, inverses):
    steps = inverses.shape[0]
    blocks = factor.shape[0]
    width = factor.shape[3]
    quarter = rhs.shape[3]
    nrhs = rhs.shape[4]
    row_count = lax.axis_size("row")
    col_count = lax.axis_size("col")
    groups = col_count // steps
    row_pos = lax.axis_index("row")
    col_pos = lax.axis_index("col")
    member = col_pos // groups
    group = col_pos % groups
    block_ids = (jnp.arange(blocks, dtype=jnp.int32) * row_count + row_pos) * groups + group
    panel = factor[:, 0, 0]
    current = rhs[:, 0, 0]
    solved_list = []
    for k in range(steps):
        owner_row = k // groups
        owner_group = k % groups
        placed = lax.dynamic_update_slice(
            jnp.zeros((width, nrhs), jnp.float32),
            current[0],
            (member * quarter, jnp.zeros((), jnp.int32)),
        )
        contrib = placed
        is_owner = jnp.logical_and(row_pos == owner_row, group == owner_group)
        contrib = jnp.where(is_owner, contrib, jnp.zeros_like(contrib))
        complete = lax.psum(contrib, "col")
        solved_block = jnp.dot(inverses[k], complete, precision=lax.Precision.HIGHEST)
        solved_block = broadcast(solved_block, "row", owner_row)
        solved_list.append(solved_block)
        keep = (block_ids > k).astype(jnp.float32)[:, None, None]

        def column_update(solved_now=solved_block, keep_now=keep):
            return (
                jnp.einsum("rji,jh->rih", panel, solved_now, precision=lax.Precision.HIGHEST)
                * keep_now
            )

        def no_update():
            return jnp.zeros((blocks, width, nrhs), jnp.float32)

        update = lax.cond(member == k, column_update, no_update)
        current = current - group_reduce(update, member, steps, groups)
    stacked = jnp.stack(solved_list)
    share = width // col_count
    solved_rows = lax.dynamic_slice_in_dim(stacked, col_pos * share, share, 1)
    return (solved_rows, current[:, None, None])


def solution(mesh):
    in_specs = (P(None, "row", "col", None, None), P(None, "row", "col", None, None), P())
    out_specs = (P(None, "col", None), P(None, "row", "col", None, None))
    return jax.shard_map(
        on_device, mesh=mesh, in_specs=in_specs, out_specs=out_specs, check_vma=False
    )
```

profile of v0, /device:TPU:7, one launch (start us, length us, event | category | flops | bytes accessed | tf_op | source)
XLA Modules:
  0.0 980.9 jit_solution(4131290574086656395)
XLA Ops:
  7.2 0.0 all-reduce.9.cloned.1.call-start
  7.3 0.9 bitcast_dynamic-update-slice_fusion
  8.1 0.7 copy-done.5
  8.9 0.0 all-reduce.11.cloned.1.call-start
  9.0 6.6 copy.5
  15.6 139.2 %all-reduce.9.cloned.1.call-done = f32[512,128]{1,0:T(8,128)} async-done(((f32[512,128]{1,0:T(8,128)}), f32[512,128]{1,0:T(8,128)}) %all-reduce.9.cloned.1.call-update) | async-done | bytes 262160 | tf_op jit(solution)/shard_map/psum | solution.py:57
  154.7 3.3 fusion.7
  158.0 0.0 all-reduce.11.cloned.1.call-update
  158.0 0.0 all-reduce.13.cloned.1.call-start
  158.1 65.0 %all-reduce.11.cloned.1.call-done = f32[512,128]{0,1:T(8,128)} async-done(((f32[512,128]{0,1:T(8,128)}), f32[512,128]{0,1:T(8,128)}) %all-reduce.11.cloned.1.call-update) | async-done | bytes 262160 | tf_op jit(solution)/shard_map/psum | solution.py:15
  223.1 7.2 conditional.4
  223.1 7.2 convolution_multiply_fusion
  230.3 0.9 dynamic-slice_bitcast_fusion.11
  231.2 2.7 collective-permute-start.2
  233.8 18.1 %collective-permute-done = f32[6,128,128]{2,1,0:T(8,128)S(1)} collective-permute-done((f32[6,128,128]{2,1,0:T(8,128)}, f32[6,128,128]{2,1,0:T(8,128)S(1)}, u32[]{:S(2)}, u32[]{:S(2)}) %collective-permute-start) | collective-permute-done | bytes 393248 | tf_op jit(solution)/shard_map/ppermute | solution.py:10
  251.9 0.3 collective-permute-done.2
  252.2 1.1 fusion.28
  253.4 0.7 copy-done.6
  254.0 0.0 all-reduce.13.cloned.1.call-update
  254.1 0.0 all-reduce.15.cloned.1.call-start
  254.1 140.4 %all-reduce.13.cloned.1.call-done = f32[512,128]{1,0:T(8,128)} async-done(((f32[512,128]{1,0:T(8,128)}), f32[512,128]{1,0:T(8,128)}) %all-reduce.13.cloned.1.call-update) | async-done | bytes 262160 | tf_op jit(solution)/shard_map/psum | solution.py:57
  394.5 3.3 fusion.6
  397.8 0.0 all-reduce.17.cloned.1.call-start
  397.8 65.0 %all-reduce.15.cloned.1.call-done = f32[512,128]{0,1:T(8,128)} async-done(((f32[512,128]{0,1:T(8,128)}), f32[512,128]{0,1:T(8,128)}) %all-reduce.15.cloned.1.call-update) | async-done | bytes 262160 | tf_op jit(solution)/shard_map/psum | solution.py:15
  462.9 0.2 conditional.5
  462.9 0.2 reshape.83
  463.1 0.9 dynamic-slice_bitcast_fusion.8
  463.9 8.2 collective-permute-start.3
  472.1 2.4 collective-permute-start.5
  474.5 6.6 collective-permute-done.3
  481.1 8.3 collective-permute-done.4
  489.4 0.8 collective-permute-done.5
  490.3 1.1 fusion.25
  491.4 0.7 copy-done.7
  492.2 0.0 all-reduce.19.cloned.1.call-start
  492.2 141.5 %all-reduce.17.cloned.1.call-done = f32[512,128]{1,0:T(8,128)} async-done(((f32[512,128]{1,0:T(8,128)}), f32[512,128]{1,0:T(8,128)}) %all-reduce.17.cloned.1.call-update) | async-done | bytes 262160 | tf_op jit(solution)/shard_map/psum | solution.py:57
  633.7 3.3 fusion.5
  637.0 0.0 all-reduce.21.cloned.1.call-start
  637.0 65.1 %all-reduce.19.cloned.1.call-done = f32[512,128]{0,1:T(8,128)} async-done(((f32[512,128]{0,1:T(8,128)}), f32[512,128]{0,1:T(8,128)}) %all-reduce.19.cloned.1.call-update) | async-done | bytes 262160 | tf_op jit(solution)/shard_map/psum | solution.py:15
  702.1 0.2 conditional.6
  702.1 0.2 reshape.85
  702.3 0.9 dynamic-slice_bitcast_fusion.5
  703.1 1.2 collective-permute-start.6
  704.3 8.5 collective-permute-start.7
  712.9 2.1 collective-permute-start.8
  714.9 0.5 collective-permute-done.6
  715.4 15.7 %collective-permute-done.7 = f32[6,128,128]{2,1,0:T(8,128)S(1)} collective-permute-done((f32[6,128,128]{2,1,0:T(8,128)S(1)}, f32[6,128,128]{2,1,0:T(8,128)S(1)}, u32[]{:S(2)}, u32[]{:S(2)}) %collective-permute-start.7) | collective-permute-done | bytes 393248 | tf_op jit(solution)/shard_map/ppermute | solution.py:10
  731.1 1.1 fusion.22
  732.3 0.7 copy-done.4
  733.0 0.0 all-reduce.23.cloned.1.call-start
  733.0 141.1 %all-reduce.21.cloned.1.call-done = f32[512,128]{1,0:T(8,128)} async-done(((f32[512,128]{1,0:T(8,128)}), f32[512,128]{1,0:T(8,128)}) %all-reduce.21.cloned.1.call-update) | async-done | bytes 262160 | tf_op jit(solution)/shard_map/psum | solution.py:57
  874.1 3.3 fusion.4
  877.4 65.1 %all-reduce.23.cloned.1.call-done = f32[512,128]{0,1:T(8,128)} async-done(((f32[512,128]{0,1:T(8,128)}), f32[512,128]{0,1:T(8,128)}) %all-reduce.23.cloned.1.call-update) | async-done | bytes 262160 | tf_op jit(solution)/shard_map/psum | solution.py:15
  942.5 0.2 conditional.7
  942.5 0.2 reshape.87
  942.7 1.1 dynamic-slice_bitcast_fusion.2
  943.8 2.7 collective-permute-start.10
  946.5 6.7 collective-permute-start.11
  953.2 0.6 collective-permute-start.9
  953.8 0.1 fusion.31
  954.0 0.7 copy.10
  954.7 1.8 collective-permute-done.10
  956.5 15.5 %collective-permute-done.11 = f32[6,128,128]{2,1,0:T(8,128)} collective-permute-done((f32[6,128,128]{2,1,0:T(8,128)}, f32[6,128,128]{2,1,0:T(8,128)}, u32[]{:S(2)}, u32[]{:S(2)}) %collective-permute-start.11) | collective-permute-done | bytes 393248 | tf_op jit(solution)/shard_map/ppermute | solution.py:10
  972.0 2.1 fusion.19
  (35 shorter events, 0.3 us)
Async XLA Ops:
  7.2 147.6 %all-reduce.9.cloned.1.call-start = ((), (), s32[]{:S(2)}) async-start(), calls=%async_computation | async-start | bytes 524288 | tf_op jit(solution)/shard_map/psum | solution.py:57
  8.1 0.7 copy-start.5
  8.9 214.3 %all-reduce.11.cloned.1.call-start = ((), (), s32[]{:S(2)}) async-start(), calls=%async_computation.1 | async-start | bytes 524288 | tf_op jit(solution)/shard_map/psum | solution.py:15
  158.0 236.5 %all-reduce.13.cloned.1.call-start = ((), (), s32[]{:S(2)}) async-start(), calls=%async_computation.2 | async-start | bytes 524288 | tf_op jit(solution)/shard_map/psum | solution.py:57
  230.3 21.9 %copy-start.8 = (f32[6,1,1,128,128]{4,3,2,1,0:T(8,128)S(1)}, f32[6,1,1,128,128]{4,3,2,1,0:T(8,128)}, u32[]{:S(2)}) copy-start(f32[6,1,1,128,128]{4,3,2,1,0:T(8,128)} %param.12) | copy-start | bytes 1179652
  231.1 20.7 %collective-permute-start = (f32[6,128,128]{2,1,0:T(8,128)}, f32[6,128,128]{2,1,0:T(8,128)S(1)}, u32[]{:S(2)}, u32[]{:S(2)}) collective-permute-start(f32[6,128,128]{2,1,0:T(8,128)} %get-tuple-element.79), channel_id=1, source_target_pairs={{24,0},{25,1},{26,2},{27,3},{28,4},{29,5},{30,6},{31,7},{0,8},{1,9... | collective-permute-start | bytes 1179656 | tf_op jit(solution)/shard_map/ppermute | solution.py:10
  231.1 20.7 %collective-permute-start.1 = (f32[6,128,128]{2,1,0:T(8,128)S(1)}, f32[6,128,128]{2,1,0:T(8,128)S(1)}, u32[]{:S(2)}, u32[]{:S(2)}) collective-permute-start(f32[6,128,128]{2,1,0:T(8,128)S(1)} %get-tuple-element.81), channel_id=1, source_target_pairs={{16,0},{17,1},{18,2},{19,3},{20,4},{21,5},{22,6},{23,7},{24,8},{25... | collective-permute-start | bytes 1179656 | tf_op jit(solution)/shard_map/ppermute | solution.py:10
  231.2 21.0 %collective-permute-start.2 = (f32[6,128,128]{2,1,0:T(8,128)S(1)}, f32[6,128,128]{2,1,0:T(8,128)}, u32[]{:S(2)}, u32[]{:S(2)}) collective-permute-start(f32[6,128,128]{2,1,0:T(8,128)S(1)} %get-tuple-element.80), channel_id=1, source_target_pairs={{8,0},{9,1},{10,2},{11,3},{12,4},{13,5},{14,6},{15,7},{16,8},{17,9... | collective-permute-start | bytes 1179656 | tf_op jit(solution)/shard_map/ppermute | solution.py:10
  253.3 0.7 copy-start.6
  254.1 208.8 %all-reduce.15.cloned.1.call-start = ((), (), s32[]{:S(2)}) async-start(), calls=%async_computation.3 | async-start | bytes 524288 | tf_op jit(solution)/shard_map/psum | solution.py:15
  397.8 235.9 %all-reduce.17.cloned.1.call-start = ((), (), s32[]{:S(2)}) async-start(), calls=%async_computation.4 | async-start | bytes 524288 | tf_op jit(solution)/shard_map/psum | solution.py:57
  463.9 17.2 %collective-permute-start.3 = (f32[6,128,128]{2,1,0:T(8,128)}, f32[6,128,128]{2,1,0:T(8,128)S(1)}, u32[]{:S(2)}, u32[]{:S(2)}) collective-permute-start(f32[6,128,128]{2,1,0:T(8,128)} %get-tuple-element.76), channel_id=1, source_target_pairs={{24,0},{25,1},{26,2},{27,3},{28,4},{29,5},{30,6},{31,7},{0,8},{1,9... | collective-permute-start | bytes 1179656 | tf_op jit(solution)/shard_map/ppermute | solution.py:10
  472.1 17.3 %collective-permute-start.4 = (f32[6,128,128]{2,1,0:T(8,128)S(1)}, f32[6,128,128]{2,1,0:T(8,128)S(1)}, u32[]{:S(2)}, u32[]{:S(2)}) collective-permute-start(f32[6,128,128]{2,1,0:T(8,128)S(1)} %get-tuple-element.78), channel_id=1, source_target_pairs={{16,0},{17,1},{18,2},{19,3},{20,4},{21,5},{22,6},{23,7},{24,8},{25... | collective-permute-start | bytes 1179656 | tf_op jit(solution)/shard_map/ppermute | solution.py:10
  472.1 18.2 %collective-permute-start.5 = (f32[6,128,128]{2,1,0:T(8,128)S(1)}, f32[6,128,128]{2,1,0:T(8,128)}, u32[]{:S(2)}, u32[]{:S(2)}) collective-permute-start(f32[6,128,128]{2,1,0:T(8,128)S(1)} %get-tuple-element.77), channel_id=1, source_target_pairs={{8,0},{9,1},{10,2},{11,3},{12,4},{13,5},{14,6},{15,7},{16,8},{17,9... | collective-permute-start | bytes 1179656 | tf_op jit(solution)/shard_map/ppermute | solution.py:10
  491.4 0.7 copy-start.7
  492.2 209.9 %all-reduce.19.cloned.1.call-start = ((), (), s32[]{:S(2)}) async-start(), calls=%async_computation.5 | async-start | bytes 524288 | tf_op jit(solution)/shard_map/psum | solution.py:15
  637.0 237.1 %all-reduce.21.cloned.1.call-start = ((), (), s32[]{:S(2)}) async-start(), calls=%async_computation.6 | async-start | bytes 524288 | tf_op jit(solution)/shard_map/psum | solution.py:57
  703.1 12.3 %collective-permute-start.6 = (f32[6,128,128]{2,1,0:T(8,128)}, f32[6,128,128]{2,1,0:T(8,128)S(1)}, u32[]{:S(2)}, u32[]{:S(2)}) collective-permute-start(f32[6,128,128]{2,1,0:T(8,128)} %get-tuple-element.73), channel_id=1, source_target_pairs={{24,0},{25,1},{26,2},{27,3},{28,4},{29,5},{30,6},{31,7},{0,8},{1,9... | collective-permute-start | bytes 1179656 | tf_op jit(solution)/shard_map/ppermute | solution.py:10
  704.3 26.8 %collective-permute-start.7 = (f32[6,128,128]{2,1,0:T(8,128)S(1)}, f32[6,128,128]{2,1,0:T(8,128)S(1)}, u32[]{:S(2)}, u32[]{:S(2)}) collective-permute-start(f32[6,128,128]{2,1,0:T(8,128)S(1)} %get-tuple-element.75), channel_id=1, source_target_pairs={{16,0},{17,1},{18,2},{19,3},{20,4},{21,5},{22,6},{23,7},{24,8},{25... | collective-permute-start | bytes 1179656 | tf_op jit(solution)/shard_map/ppermute | solution.py:10
  712.9 18.2 %collective-permute-start.8 = (f32[6,128,128]{2,1,0:T(8,128)S(1)}, f32[6,128,128]{2,1,0:T(8,128)}, u32[]{:S(2)}, u32[]{:S(2)}) collective-permute-start(f32[6,128,128]{2,1,0:T(8,128)S(1)} %get-tuple-element.74), channel_id=1, source_target_pairs={{8,0},{9,1},{10,2},{11,3},{12,4},{13,5},{14,6},{15,7},{16,8},{17,9... | collective-permute-start | bytes 1179656 | tf_op jit(solution)/shard_map/ppermute | solution.py:10
  732.2 0.7 copy-start.4
  733.0 209.5 %all-reduce.23.cloned.1.call-start = ((), (), s32[]{:S(2)}) async-start(), calls=%async_computation.7 | async-start | bytes 524288 | tf_op jit(solution)/shard_map/psum | solution.py:15
  942.7 11.1 %copy-start = (f32[512,128]{0,1:T(8,128)S(1)}, f32[512,128]{0,1:T(8,128)}, u32[]{:S(2)}) copy-start(f32[512,128]{0,1:T(8,128)} %all-reduce.11.cloned.1.call-done) | copy-start | bytes 786436
  942.7 11.1 %copy-start.1 = (f32[512,128]{0,1:T(8,128)S(1)}, f32[512,128]{0,1:T(8,128)}, u32[]{:S(2)}) copy-start(f32[512,128]{0,1:T(8,128)} %all-reduce.15.cloned.1.call-done) | copy-start | bytes 786436
  942.7 11.1 %copy-start.2 = (f32[512,128]{0,1:T(8,128)S(1)}, f32[512,128]{0,1:T(8,128)}, u32[]{:S(2)}) copy-start(f32[512,128]{0,1:T(8,128)} %all-reduce.19.cloned.1.call-done) | copy-start | bytes 786436
  942.7 11.1 %copy-start.3 = (f32[512,128]{0,1:T(8,128)S(1)}, f32[512,128]{0,1:T(8,128)}, u32[]{:S(2)}) copy-start(f32[512,128]{0,1:T(8,128)} %all-reduce.23.cloned.1.call-done) | copy-start | bytes 786436
  943.8 12.7 %collective-permute-start.10 = (f32[6,128,128]{2,1,0:T(8,128)}, f32[6,128,128]{2,1,0:T(8,128)}, u32[]{:S(2)}, u32[]{:S(2)}) collective-permute-start(f32[6,128,128]{2,1,0:T(8,128)} %get-tuple-element.72), channel_id=1, source_target_pairs={{16,0},{17,1},{18,2},{19,3},{20,4},{21,5},{22,6},{23,7},{24,8},{25... | collective-permute-start | bytes 1179656 | tf_op jit(solution)/shard_map/ppermute | solution.py:10
  946.5 25.5 %collective-permute-start.11 = (f32[6,128,128]{2,1,0:T(8,128)}, f32[6,128,128]{2,1,0:T(8,128)}, u32[]{:S(2)}, u32[]{:S(2)}) collective-permute-start(f32[6,128,128]{2,1,0:T(8,128)} %get-tuple-element.71), channel_id=1, source_target_pairs={{8,0},{9,1},{10,2},{11,3},{12,4},{13,5},{14,6},{15,7},{16,8},{17,9... | collective-permute-start | bytes 1179656 | tf_op jit(solution)/shard_map/ppermute | solution.py:10
  953.2 18.8 %collective-permute-start.9 = (f32[6,128,128]{2,1,0:T(8,128)}, f32[6,128,128]{2,1,0:T(8,128)}, u32[]{:S(2)}, u32[]{:S(2)}) collective-permute-start(f32[6,128,128]{2,1,0:T(8,128)} %get-tuple-element.70), channel_id=1, source_target_pairs={{24,0},{25,1},{26,2},{27,3},{28,4},{29,5},{30,6},{31,7},{0,8},{1,9... | collective-permute-start | bytes 1179656 | tf_op jit(solution)/shard_map/ppermute | solution.py:10
Sparse Core Ops, SparseCore 0:
  12.0 142.6 all-reduce.8
  158.1 64.9 all-reduce.10
  254.2 140.2 all-reduce.12
  397.9 64.9 all-reduce.14
  492.3 141.3 all-reduce.16
  637.1 64.9 all-reduce.18
  733.1 140.9 all-reduce.20
  877.5 64.9 all-reduce.22
where the time goes:
time: 981 us
  waiting for transfers between devices  890 us (91%)
  starting transfers between devices  35.4 us (4%)
  matrix products  20.2 us (2%)
  between operations  14.4 us (1%)
  local copies, waits for them, and re-layouts  14.3 us (1%)
    psum x4, waiting for transfers between devices, on_device(): complete = lax.psum(contrib, 'col')  562 us
    psum x4, waiting for transfers between devices, broadcast(): return lax.psum(jnp.where(mine, x, jnp.zeros_like(x)), axis)  260 us
    ppermute x12, waiting for transfers between devices, shifted(): return lax.ppermute(block, axis, route)  67.6 us
    ppermute x12, starting transfers between devices, shifted(): return lax.ppermute(block, axis, route)  35.1 us
  transfers between devices with their start and end apart: 20, of which 17 were waited for; matrix products, arithmetic and copies ran while one was open for 1% of the time, Pallas kernels for 0%

commit v1 on v0

--- a/solution.py
+++ b/solution.py
@@ -54,7 +54,13 @@
         contrib = placed
         is_owner = jnp.logical_and(row_pos == owner_row, group == owner_group)
         contrib = jnp.where(is_owner, contrib, jnp.zeros_like(contrib))
-        complete = lax.psum(contrib, "col")
+        devices_2 = lax.axis_size("col")
+        complete, far = (contrib, 1)
+        while far < devices_2:
+            complete = complete + lax.ppermute(
+                complete, "col", [(i_2, i_2 ^ far) for i_2 in range(devices_2)]
+            )
+            far = 2 * far
         solved_block = jnp.dot(inverses[k], complete, precision=lax.Precision.HIGHEST)
         solved_block = broadcast(solved_block, "row", owner_row)
         solved_list.append(solved_block)

time: 981 us -> 635 us (0.65)
  waiting for transfers between devices: 890 us -> 475 us
  starting transfers between devices: 35.4 us -> 97.1 us
    psum x4 -> x0, waiting for transfers between devices: 562 us -> none  [on_device(): complete = lax.psum(contrib, 'col')]
    ppermute x0 -> x20, waiting for transfers between devices: none -> 139 us  [on_device(): lax.ppermute(complete, 'col', [(i_2, i_2 ^ far) for i_2 in range(devices_...]
    ppermute x0 -> x20, starting transfers between devices: none -> 61.2 us  [on_device(): lax.ppermute(complete, 'col', [(i_2, i_2 ^ far) for i_2 in range(devices_...]
  transfers between devices with their start and end apart: 20 -> 36, of which waited for: 17 -> 32; matrix products, arithmetic and copies ran while one was open for 1% -> 1% of each run, Pallas kernels for 0% -> 0%
where the time goes in v1:
time: 635 us; the launch traced here: 626 us
  waiting for transfers between devices  475 us (75%)
  starting transfers between devices  97.1 us (15%)
  matrix products  19.9 us (3%)
  between operations  14.5 us (2%)
  local copies, waits for them, and re-layouts  11.5 us (2%)
  other arithmetic  7.63 us (1%)
    psum x4, waiting for transfers between devices, broadcast(): return lax.psum(jnp.where(mine, x, jnp.zeros_like(x)), axis)  268 us
    ppermute x20, waiting for transfers between devices, on_device(): lax.ppermute(complete, 'col', [(i_2, i_2 ^ far) for i_2 in range(devices_...  139 us
    ppermute x12, waiting for transfers between devices, shifted(): return lax.ppermute(block, axis, route)  67.6 us
    ppermute x20, starting transfers between devices, on_device(): lax.ppermute(complete, 'col', [(i_2, i_2 ^ far) for i_2 in range(devices_...  61.2 us
    ppermute x12, starting transfers between devices, shifted(): return lax.ppermute(block, axis, route)  35.7 us
    dot_general x4, matrix products, on_device(): jnp.dot(inverses[k], complete, precision=lax.Precision.HIGHEST)  12.7 us
  transfers between devices with their start and end apart: 36, of which 32 were waited for; matrix products, arithmetic and copies ran while one was open for 1% of the time, Pallas kernels for 0%

profile of v1, /device:TPU:7, one launch (start us, length us, event | category | flops | bytes accessed | tf_op | source)
XLA Modules:
  0.0 625.8 jit_solution(10397072337889971793)
XLA Ops:
  8.1 1.6 collective-permute-start
  9.8 5.9 collective-permute-done
  16.5 3.1 collective-permute-start.1
  19.6 11.3 %collective-permute-done.1 = f32[512,128]{1,0:T(8,128)S(1)} collective-permute-done((f32[512,128]{1,0:T(8,128)S(1)}, f32[512,128]{1,0:T(8,128)S(1)}, u32[]{:S(2)}, u32[]{:S(2)}) %collective-permute-start.1) | collective-permute-done | bytes 262176 | tf_op jit(solution)/shard_map/ppermute | solution.py:60
  31.0 6.5 %collective-permute-start.2 = (f32[512,128]{1,0:T(8,128)S(1)}, f32[512,128]{1,0:T(8,128)S(1)}, u32[]{:S(2)}, u32[]{:S(2)}) collective-permute-start(f32[512,128]{1,0:T(8,128)S(1)} %add.236), channel_id=1, source_target_pairs={{0,4},{1,5},{2,6},{3,7},{4,0},{5,1},{6,2},{7,3},{8,12},{9,13},{10,... | collective-permute-start | bytes 786440 | tf_op jit(solution)/shard_map/ppermute | solution.py:60
  37.5 8.6 %collective-permute-done.2 = f32[512,128]{1,0:T(8,128)S(1)} collective-permute-done((f32[512,128]{1,0:T(8,128)S(1)}, f32[512,128]{1,0:T(8,128)S(1)}, u32[]{:S(2)}, u32[]{:S(2)}) %collective-permute-start.2) | collective-permute-done | bytes 262176 | tf_op jit(solution)/shard_map/ppermute | solution.py:60
  46.1 1.4 collective-permute-start.3
  47.5 3.9 collective-permute-done.3
  51.5 3.0 collective-permute-start.4
  54.5 6.6 %copy.5 = f32[6,1,1,512,512]{3,4,0,2,1:T(8,128)} copy(f32[6,1,1,512,512]{4,3,2,1,0:T(8,128)} %param.11) | data formatting | bytes 12582912 | tf_op args[0]
  61.0 3.2 fusion.7
  64.3 68.1 %all-reduce.5.cloned.1.call-done = f32[512,128]{0,1:T(8,128)} async-done(((f32[512,128]{0,1:T(8,128)}), f32[512,128]{0,1:T(8,128)}) %all-reduce.5.cloned.1.call-update) | async-done | bytes 262160 | tf_op jit(solution)/shard_map/psum | solution.py:15
  132.4 7.2 %conditional.4 = (f32[6,4,128,128]{3,2,1,0:T(8,128)S(1)}) conditional(s32[]{:T(128)} %convert_element_type.52, () %tuple.40, (f32[6,512,512]{1,2,0:T(8,128)}, f32[512,128]{0,1:T(8,128)}, f32[6,1,1]{0,2,1:T(1,128)S(1)}) %tuple.81), branch_computations={%region_1.2_spmd, %region_2.3_spmd} | conditional | flops 2416312320 | bytes 8126496 | solution.py:78
  132.4 7.2 %convolution_multiply_fusion = f32[6,512,128]{2,1,0:T(8,128)S(1)} fusion(f32[6,512,512]{1,2,0:T(8,128)} %get-tuple-element.40, f32[6]{0:T(128)S(1)} %bitcast.149, f32[512,128]{0,1:T(8,128)} %get-tuple-element.55), kind=kOutput, calls=%fused_computation | convolution fusion | flops 2416312320 | bytes 8126488 | tf_op jit(solution)/shard_map/cond/branch_1_fun/rji,jh->rih/dot_general | solution.py:71
  140.5 2.7 collective-permute-start.7
  143.2 18.1 %collective-permute-done.5 = f32[6,128,128]{2,1,0:T(8,128)S(1)} collective-permute-done((f32[6,128,128]{2,1,0:T(8,128)}, f32[6,128,128]{2,1,0:T(8,128)S(1)}, u32[]{:S(2)}, u32[]{:S(2)}) %collective-permute-start.5) | collective-permute-done | bytes 393248 | tf_op jit(solution)/shard_map/ppermute | solution.py:10
  162.7 1.4 collective-permute-start.8
  164.0 5.7 collective-permute-done.8
  169.7 2.4 collective-permute-start.9
  172.1 11.4 %collective-permute-done.9 = f32[512,128]{1,0:T(8,128)S(1)} collective-permute-done((f32[512,128]{1,0:T(8,128)S(1)}, f32[512,128]{1,0:T(8,128)S(1)}, u32[]{:S(2)}, u32[]{:S(2)}) %collective-permute-start.9) | collective-permute-done | bytes 262176 | tf_op jit(solution)/shard_map/ppermute | solution.py:60
  183.6 6.4 %collective-permute-start.10 = (f32[512,128]{1,0:T(8,128)S(1)}, f32[512,128]{1,0:T(8,128)S(1)}, u32[]{:S(2)}, u32[]{:S(2)}) collective-permute-start(f32[512,128]{1,0:T(8,128)S(1)} %add.258), channel_id=1, source_target_pairs={{0,4},{1,5},{2,6},{3,7},{4,0},{5,1},{6,2},{7,3},{8,12},{9,13},{10,... | collective-permute-start | bytes 786440 | tf_op jit(solution)/shard_map/ppermute | solution.py:60
  190.0 8.8 %collective-permute-done.10 = f32[512,128]{1,0:T(8,128)S(1)} collective-permute-done((f32[512,128]{1,0:T(8,128)S(1)}, f32[512,128]{1,0:T(8,128)S(1)}, u32[]{:S(2)}, u32[]{:S(2)}) %collective-permute-start.10) | collective-permute-done | bytes 262176 | tf_op jit(solution)/shard_map/ppermute | solution.py:60
  198.8 1.2 collective-permute-start.11
  199.9 4.3 collective-permute-done.11
  204.3 2.2 collective-permute-start.12
  206.5 7.3 %collective-permute-done.12 = f32[512,128]{1,0:T(8,128)S(1)} collective-permute-done((f32[512,128]{1,0:T(8,128)S(1)}, f32[512,128]{1,0:T(8,128)S(1)}, u32[]{:S(2)}, u32[]{:S(2)}) %collective-permute-start.12) | collective-permute-done | bytes 262176 | tf_op jit(solution)/shard_map/ppermute | solution.py:60
  213.8 3.2 fusion.6
  217.1 66.9 %all-reduce.7.cloned.1.call-done = f32[512,128]{0,1:T(8,128)} async-done(((f32[512,128]{0,1:T(8,128)}), f32[512,128]{0,1:T(8,128)}) %all-reduce.7.cloned.1.call-update) | async-done | bytes 262160 | tf_op jit(solution)/shard_map/psum | solution.py:15
  285.0 8.2 %collective-permute-start.13 = (f32[6,128,128]{2,1,0:T(8,128)}, f32[6,128,128]{2,1,0:T(8,128)S(1)}, u32[]{:S(2)}, u32[]{:S(2)}) collective-permute-start(f32[6,128,128]{2,1,0:T(8,128)} %get-tuple-element.76), channel_id=1, source_target_pairs={{24,0},{25,1},{26,2},{27,3},{28,4},{29,5},{30,6},{31,7},{0,8},{1,9... | collective-permute-start | bytes 1179656 | tf_op jit(solution)/shard_map/ppermute | solution.py:10
  293.2 2.4 collective-permute-start.15
  295.6 6.6 %collective-permute-done.13 = f32[6,128,128]{2,1,0:T(8,128)S(1)} collective-permute-done((f32[6,128,128]{2,1,0:T(8,128)}, f32[6,128,128]{2,1,0:T(8,128)S(1)}, u32[]{:S(2)}, u32[]{:S(2)}) %collective-permute-start.13) | collective-permute-done | bytes 393248 | tf_op jit(solution)/shard_map/ppermute | solution.py:10
  302.2 8.3 %collective-permute-done.14 = f32[6,128,128]{2,1,0:T(8,128)S(1)} collective-permute-done((f32[6,128,128]{2,1,0:T(8,128)S(1)}, f32[6,128,128]{2,1,0:T(8,128)S(1)}, u32[]{:S(2)}, u32[]{:S(2)}) %collective-permute-start.14) | collective-permute-done | bytes 393248 | tf_op jit(solution)/shard_map/ppermute | solution.py:10
  312.5 1.4 collective-permute-start.16
  313.9 6.2 collective-permute-done.16
  320.1 2.3 collective-permute-start.17
  322.5 11.4 %collective-permute-done.17 = f32[512,128]{1,0:T(8,128)S(1)} collective-permute-done((f32[512,128]{1,0:T(8,128)S(1)}, f32[512,128]{1,0:T(8,128)S(1)}, u32[]{:S(2)}, u32[]{:S(2)}) %collective-permute-start.17) | collective-permute-done | bytes 262176 | tf_op jit(solution)/shard_map/ppermute | solution.py:60
  333.9 6.5 %collective-permute-start.18 = (f32[512,128]{1,0:T(8,128)S(1)}, f32[512,128]{1,0:T(8,128)S(1)}, u32[]{:S(2)}, u32[]{:S(2)}) collective-permute-start(f32[512,128]{1,0:T(8,128)S(1)} %add.266), channel_id=1, source_target_pairs={{0,4},{1,5},{2,6},{3,7},{4,0},{5,1},{6,2},{7,3},{8,12},{9,13},{10,... | collective-permute-start | bytes 786440 | tf_op jit(solution)/shard_map/ppermute | solution.py:60
  340.4 8.8 %collective-permute-done.18 = f32[512,128]{1,0:T(8,128)S(1)} collective-permute-done((f32[512,128]{1,0:T(8,128)S(1)}, f32[512,128]{1,0:T(8,128)S(1)}, u32[]{:S(2)}, u32[]{:S(2)}) %collective-permute-start.18) | collective-permute-done | bytes 262176 | tf_op jit(solution)/shard_map/ppermute | solution.py:60
  349.3 2.1 collective-permute-start.19
  351.4 3.8 collective-permute-done.19
  355.2 6.7 %collective-permute-start.20 = (f32[512,128]{1,0:T(8,128)S(1)}, f32[512,128]{1,0:T(8,128)S(1)}, u32[]{:S(2)}, u32[]{:S(2)}) collective-permute-start(f32[512,128]{1,0:T(8,128)S(1)} %add.268), channel_id=1, source_target_pairs={{0,16},{1,17},{2,18},{3,19},{4,20},{5,21},{6,22},{7,23},{8,24},{9,... | collective-permute-start | bytes 786440 | tf_op jit(solution)/shard_map/ppermute | solution.py:60
  361.9 3.8 collective-permute-done.20
  365.7 3.2 fusion.5
  368.9 65.9 %all-reduce.9.cloned.1.call-done = f32[512,128]{0,1:T(8,128)} async-done(((f32[512,128]{0,1:T(8,128)}), f32[512,128]{0,1:T(8,128)}) %all-reduce.9.cloned.1.call-update) | async-done | bytes 262160 | tf_op jit(solution)/shard_map/psum | solution.py:15
  436.1 1.2 collective-permute-start.21
  437.3 8.5 %collective-permute-start.22 = (f32[6,128,128]{2,1,0:T(8,128)S(1)}, f32[6,128,128]{2,1,0:T(8,128)S(1)}, u32[]{:S(2)}, u32[]{:S(2)}) collective-permute-start(f32[6,128,128]{2,1,0:T(8,128)S(1)} %get-tuple-element.75), channel_id=1, source_target_pairs={{16,0},{17,1},{18,2},{19,3},{20,4},{21,5},{22,6},{23,7},{24,8},{25... | collective-permute-start | bytes 1179656 | tf_op jit(solution)/shard_map/ppermute | solution.py:10
  445.8 2.1 collective-permute-start.23
  448.4 15.7 %collective-permute-done.22 = f32[6,128,128]{2,1,0:T(8,128)S(1)} collective-permute-done((f32[6,128,128]{2,1,0:T(8,128)S(1)}, f32[6,128,128]{2,1,0:T(8,128)S(1)}, u32[]{:S(2)}, u32[]{:S(2)}) %collective-permute-start.22) | collective-permute-done | bytes 393248 | tf_op jit(solution)/shard_map/ppermute | solution.py:10
  465.2 1.4 collective-permute-start.24
  466.6 6.2 collective-permute-done.24
  472.8 2.4 collective-permute-start.25
  475.2 11.4 %collective-permute-done.25 = f32[512,128]{1,0:T(8,128)S(1)} collective-permute-done((f32[512,128]{1,0:T(8,128)S(1)}, f32[512,128]{1,0:T(8,128)S(1)}, u32[]{:S(2)}, u32[]{:S(2)}) %collective-permute-start.25) | collective-permute-done | bytes 262176 | tf_op jit(solution)/shard_map/ppermute | solution.py:60
  486.6 6.5 %collective-permute-start.26 = (f32[512,128]{1,0:T(8,128)S(1)}, f32[512,128]{1,0:T(8,128)S(1)}, u32[]{:S(2)}, u32[]{:S(2)}) collective-permute-start(f32[512,128]{1,0:T(8,128)S(1)} %add.274), channel_id=1, source_target_pairs={{0,4},{1,5},{2,6},{3,7},{4,0},{5,1},{6,2},{7,3},{8,12},{9,13},{10,... | collective-permute-start | bytes 786440 | tf_op jit(solution)/shard_map/ppermute | solution.py:60
  493.1 8.8 %collective-permute-done.26 = f32[512,128]{1,0:T(8,128)S(1)} collective-permute-done((f32[512,128]{1,0:T(8,128)S(1)}, f32[512,128]{1,0:T(8,128)S(1)}, u32[]{:S(2)}, u32[]{:S(2)}) %collective-permute-start.26) | collective-permute-done | bytes 262176 | tf_op jit(solution)/shard_map/ppermute | solution.py:60
  502.3 5.0 collective-permute-done.27
  507.3 2.5 collective-permute-start.28
  509.8 6.5 %collective-permute-done.28 = f32[512,128]{1,0:T(8,128)S(1)} collective-permute-done((f32[512,128]{1,0:T(8,128)S(1)}, f32[512,128]{1,0:T(8,128)S(1)}, u32[]{:S(2)}, u32[]{:S(2)}) %collective-permute-start.28) | collective-permute-done | bytes 262176 | tf_op jit(solution)/shard_map/ppermute | solution.py:60
  516.2 3.2 fusion.4
  519.5 67.2 %all-reduce.11.cloned.1.call-done = f32[512,128]{0,1:T(8,128)} async-done(((f32[512,128]{0,1:T(8,128)}), f32[512,128]{0,1:T(8,128)}) %all-reduce.11.cloned.1.call-update) | async-done | bytes 262160 | tf_op jit(solution)/shard_map/psum | solution.py:15
  588.0 1.2 collective-permute-start.29
  589.2 9.4 %collective-permute-start.30 = (f32[6,128,128]{2,1,0:T(8,128)}, f32[6,128,128]{2,1,0:T(8,128)}, u32[]{:S(2)}, u32[]{:S(2)}) collective-permute-start(f32[6,128,128]{2,1,0:T(8,128)} %get-tuple-element.72), channel_id=1, source_target_pairs={{16,0},{17,1},{18,2},{19,3},{20,4},{21,5},{22,6},{23,7},{24,8},{25... | collective-permute-start | bytes 1179656 | tf_op jit(solution)/shard_map/ppermute | solution.py:10
  599.5 7.8 %collective-permute-done.29 = f32[6,128,128]{2,1,0:T(8,128)} collective-permute-done((f32[6,128,128]{2,1,0:T(8,128)}, f32[6,128,128]{2,1,0:T(8,128)}, u32[]{:S(2)}, u32[]{:S(2)}) %collective-permute-start.29) | collective-permute-done | bytes 393248 | tf_op jit(solution)/shard_map/ppermute | solution.py:10
  607.3 9.4 %collective-permute-done.30 = f32[6,128,128]{2,1,0:T(8,128)} collective-permute-done((f32[6,128,128]{2,1,0:T(8,128)}, f32[6,128,128]{2,1,0:T(8,128)}, u32[]{:S(2)}, u32[]{:S(2)}) %collective-permute-start.30) | collective-permute-done | bytes 393248 | tf_op jit(solution)/shard_map/ppermute | solution.py:10
  616.8 2.1 fusion.19
  (71 shorter events, 13.4 us)
Async XLA Ops:
  7.2 125.3 %all-reduce.5.cloned.1.call-start = ((), (), s32[]{:S(2)}) async-start(), calls=%async_computation | async-start | bytes 524288 | tf_op jit(solution)/shard_map/psum | solution.py:15
  8.1 7.5 %collective-permute-start = (f32[512,128]{1,0:T(8,128)S(1)}, f32[512,128]{1,0:T(8,128)S(1)}, u32[]{:S(2)}, u32[]{:S(2)}) collective-permute-start(f32[512,128]{1,0:T(8,128)S(1)} %bitcast_dynamic-update-slice_fusion), channel_id=1, source_target_pairs={{0,1},{1,0},{2,3},{3,2},{4,5},{5,4},{6,7},{7,6},{8,9},{9,8},{10,11... | collective-permute-start | bytes 786440 | tf_op jit(solution)/shard_map/ppermute | solution.py:60
  16.5 14.4 %collective-permute-start.1 = (f32[512,128]{1,0:T(8,128)S(1)}, f32[512,128]{1,0:T(8,128)S(1)}, u32[]{:S(2)}, u32[]{:S(2)}) collective-permute-start(f32[512,128]{1,0:T(8,128)S(1)} %fusion.39), channel_id=1, source_target_pairs={{0,2},{1,3},{2,0},{3,1},{4,6},{5,7},{6,4},{7,5},{8,10},{9,11},{10,... | collective-permute-start | bytes 786440 | tf_op jit(solution)/shard_map/ppermute | solution.py:60
  31.0 15.1 %collective-permute-start.2 = (f32[512,128]{1,0:T(8,128)S(1)}, f32[512,128]{1,0:T(8,128)S(1)}, u32[]{:S(2)}, u32[]{:S(2)}) collective-permute-start(f32[512,128]{1,0:T(8,128)S(1)} %add.236), channel_id=1, source_target_pairs={{0,4},{1,5},{2,6},{3,7},{4,0},{5,1},{6,2},{7,3},{8,12},{9,13},{10,... | collective-permute-start | bytes 786440 | tf_op jit(solution)/shard_map/ppermute | solution.py:60
  46.1 5.3 collective-permute-start.3
  51.5 9.6 %collective-permute-start.4 = (f32[512,128]{1,0:T(8,128)S(1)}, f32[512,128]{1,0:T(8,128)S(1)}, u32[]{:S(2)}, u32[]{:S(2)}) collective-permute-start(f32[512,128]{1,0:T(8,128)S(1)} %add.238), channel_id=1, source_target_pairs={{0,16},{1,17},{2,18},{3,19},{4,20},{5,21},{6,22},{7,23},{8,24},{9,... | collective-permute-start | bytes 786440 | tf_op jit(solution)/shard_map/ppermute | solution.py:60
  64.2 219.7 %all-reduce.7.cloned.1.call-start = ((), (), s32[]{:S(2)}) async-start(), calls=%async_computation.1 | async-start | bytes 524288 | tf_op jit(solution)/shard_map/psum | solution.py:15
  139.6 21.9 %copy-start.4 = (f32[6,1,1,128,128]{4,3,2,1,0:T(8,128)S(1)}, f32[6,1,1,128,128]{4,3,2,1,0:T(8,128)}, u32[]{:S(2)}) copy-start(f32[6,1,1,128,128]{4,3,2,1,0:T(8,128)} %param.12) | copy-start | bytes 1179652
  140.5 20.7 %collective-permute-start.5 = (f32[6,128,128]{2,1,0:T(8,128)}, f32[6,128,128]{2,1,0:T(8,128)S(1)}, u32[]{:S(2)}, u32[]{:S(2)}) collective-permute-start(f32[6,128,128]{2,1,0:T(8,128)} %get-tuple-element.79), channel_id=1, source_target_pairs={{24,0},{25,1},{26,2},{27,3},{28,4},{29,5},{30,6},{31,7},{0,8},{1,9... | collective-permute-start | bytes 1179656 | tf_op jit(solution)/shard_map/ppermute | solution.py:10
  140.5 20.7 %collective-permute-start.6 = (f32[6,128,128]{2,1,0:T(8,128)S(1)}, f32[6,128,128]{2,1,0:T(8,128)S(1)}, u32[]{:S(2)}, u32[]{:S(2)}) collective-permute-start(f32[6,128,128]{2,1,0:T(8,128)S(1)} %get-tuple-element.81), channel_id=1, source_target_pairs={{16,0},{17,1},{18,2},{19,3},{20,4},{21,5},{22,6},{23,7},{24,8},{25... | collective-permute-start | bytes 1179656 | tf_op jit(solution)/shard_map/ppermute | solution.py:10
  140.5 21.0 %collective-permute-start.7 = (f32[6,128,128]{2,1,0:T(8,128)S(1)}, f32[6,128,128]{2,1,0:T(8,128)}, u32[]{:S(2)}, u32[]{:S(2)}) collective-permute-start(f32[6,128,128]{2,1,0:T(8,128)S(1)} %get-tuple-element.80), channel_id=1, source_target_pairs={{8,0},{9,1},{10,2},{11,3},{12,4},{13,5},{14,6},{15,7},{16,8},{17,9... | collective-permute-start | bytes 1179656 | tf_op jit(solution)/shard_map/ppermute | solution.py:10
  162.7 7.1 %collective-permute-start.8 = (f32[512,128]{1,0:T(8,128)S(1)}, f32[512,128]{1,0:T(8,128)S(1)}, u32[]{:S(2)}, u32[]{:S(2)}) collective-permute-start(f32[512,128]{1,0:T(8,128)S(1)} %fusion.40), channel_id=1, source_target_pairs={{0,1},{1,0},{2,3},{3,2},{4,5},{5,4},{6,7},{7,6},{8,9},{9,8},{10,11... | collective-permute-start | bytes 786440 | tf_op jit(solution)/shard_map/ppermute | solution.py:60
  169.7 13.8 %collective-permute-start.9 = (f32[512,128]{1,0:T(8,128)S(1)}, f32[512,128]{1,0:T(8,128)S(1)}, u32[]{:S(2)}, u32[]{:S(2)}) collective-permute-start(f32[512,128]{1,0:T(8,128)S(1)} %add_dynamic-update-slice_fusion.2), channel_id=1, source_target_pairs={{0,2},{1,3},{2,0},{3,1},{4,6},{5,7},{6,4},{7,5},{8,10},{9,11},{10,... | collective-permute-start | bytes 786440 | tf_op jit(solution)/shard_map/ppermute | solution.py:60
  183.6 15.2 %collective-permute-start.10 = (f32[512,128]{1,0:T(8,128)S(1)}, f32[512,128]{1,0:T(8,128)S(1)}, u32[]{:S(2)}, u32[]{:S(2)}) collective-permute-start(f32[512,128]{1,0:T(8,128)S(1)} %add.258), channel_id=1, source_target_pairs={{0,4},{1,5},{2,6},{3,7},{4,0},{5,1},{6,2},{7,3},{8,12},{9,13},{10,... | collective-permute-start | bytes 786440 | tf_op jit(solution)/shard_map/ppermute | solution.py:60
  198.8 5.5 collective-permute-start.11
  204.3 9.5 %collective-permute-start.12 = (f32[512,128]{1,0:T(8,128)S(1)}, f32[512,128]{1,0:T(8,128)S(1)}, u32[]{:S(2)}, u32[]{:S(2)}) collective-permute-start(f32[512,128]{1,0:T(8,128)S(1)} %add.260), channel_id=1, source_target_pairs={{0,16},{1,17},{2,18},{3,19},{4,20},{5,21},{6,22},{7,23},{8,24},{9,... | collective-permute-start | bytes 786440 | tf_op jit(solution)/shard_map/ppermute | solution.py:60
  217.0 217.8 %all-reduce.9.cloned.1.call-start = ((), (), s32[]{:S(2)}) async-start(), calls=%async_computation.2 | async-start | bytes 524288 | tf_op jit(solution)/shard_map/psum | solution.py:15
  285.0 17.2 %collective-permute-start.13 = (f32[6,128,128]{2,1,0:T(8,128)}, f32[6,128,128]{2,1,0:T(8,128)S(1)}, u32[]{:S(2)}, u32[]{:S(2)}) collective-permute-start(f32[6,128,128]{2,1,0:T(8,128)} %get-tuple-element.76), channel_id=1, source_target_pairs={{24,0},{25,1},{26,2},{27,3},{28,4},{29,5},{30,6},{31,7},{0,8},{1,9... | collective-permute-start | bytes 1179656 | tf_op jit(solution)/shard_map/ppermute | solution.py:10
  293.2 17.3 %collective-permute-start.14 = (f32[6,128,128]{2,1,0:T(8,128)S(1)}, f32[6,128,128]{2,1,0:T(8,128)S(1)}, u32[]{:S(2)}, u32[]{:S(2)}) collective-permute-start(f32[6,128,128]{2,1,0:T(8,128)S(1)} %get-tuple-element.78), channel_id=1, source_target_pairs={{16,0},{17,1},{18,2},{19,3},{20,4},{21,5},{22,6},{23,7},{24,8},{25... | collective-permute-start | bytes 1179656 | tf_op jit(solution)/shard_map/ppermute | solution.py:10
  293.2 18.2 %collective-permute-start.15 = (f32[6,128,128]{2,1,0:T(8,128)S(1)}, f32[6,128,128]{2,1,0:T(8,128)}, u32[]{:S(2)}, u32[]{:S(2)}) collective-permute-start(f32[6,128,128]{2,1,0:T(8,128)S(1)} %get-tuple-element.77), channel_id=1, source_target_pairs={{8,0},{9,1},{10,2},{11,3},{12,4},{13,5},{14,6},{15,7},{16,8},{17,9... | collective-permute-start | bytes 1179656 | tf_op jit(solution)/shard_map/ppermute | solution.py:10
  312.5 7.6 %collective-permute-start.16 = (f32[512,128]{1,0:T(8,128)S(1)}, f32[512,128]{1,0:T(8,128)S(1)}, u32[]{:S(2)}, u32[]{:S(2)}) collective-permute-start(f32[512,128]{1,0:T(8,128)S(1)} %fusion.41), channel_id=1, source_target_pairs={{0,1},{1,0},{2,3},{3,2},{4,5},{5,4},{6,7},{7,6},{8,9},{9,8},{10,11... | collective-permute-start | bytes 786440 | tf_op jit(solution)/shard_map/ppermute | solution.py:60
  320.1 13.8 %collective-permute-start.17 = (f32[512,128]{1,0:T(8,128)S(1)}, f32[512,128]{1,0:T(8,128)S(1)}, u32[]{:S(2)}, u32[]{:S(2)}) collective-permute-start(f32[512,128]{1,0:T(8,128)S(1)} %add_dynamic-update-slice_fusion.1), channel_id=1, source_target_pairs={{0,2},{1,3},{2,0},{3,1},{4,6},{5,7},{6,4},{7,5},{8,10},{9,11},{10,... | collective-permute-start | bytes 786440 | tf_op jit(solution)/shard_map/ppermute | solution.py:60
  333.9 15.3 %collective-permute-start.18 = (f32[512,128]{1,0:T(8,128)S(1)}, f32[512,128]{1,0:T(8,128)S(1)}, u32[]{:S(2)}, u32[]{:S(2)}) collective-permute-start(f32[512,128]{1,0:T(8,128)S(1)} %add.266), channel_id=1, source_target_pairs={{0,4},{1,5},{2,6},{3,7},{4,0},{5,1},{6,2},{7,3},{8,12},{9,13},{10,... | collective-permute-start | bytes 786440 | tf_op jit(solution)/shard_map/ppermute | solution.py:60
  349.3 5.9 collective-permute-start.19
  355.2 10.5 %collective-permute-start.20 = (f32[512,128]{1,0:T(8,128)S(1)}, f32[512,128]{1,0:T(8,128)S(1)}, u32[]{:S(2)}, u32[]{:S(2)}) collective-permute-start(f32[512,128]{1,0:T(8,128)S(1)} %add.268), channel_id=1, source_target_pairs={{0,16},{1,17},{2,18},{3,19},{4,20},{5,21},{6,22},{7,23},{8,24},{9,... | collective-permute-start | bytes 786440 | tf_op jit(solution)/shard_map/ppermute | solution.py:60
  368.9 217.8 %all-reduce.11.cloned.1.call-start = ((), (), s32[]{:S(2)}) async-start(), calls=%async_computation.3 | async-start | bytes 524288 | tf_op jit(solution)/shard_map/psum | solution.py:15
  436.1 12.3 %collective-permute-start.21 = (f32[6,128,128]{2,1,0:T(8,128)}, f32[6,128,128]{2,1,0:T(8,128)S(1)}, u32[]{:S(2)}, u32[]{:S(2)}) collective-permute-start(f32[6,128,128]{2,1,0:T(8,128)} %get-tuple-element.73), channel_id=1, source_target_pairs={{24,0},{25,1},{26,2},{27,3},{28,4},{29,5},{30,6},{31,7},{0,8},{1,9... | collective-permute-start | bytes 1179656 | tf_op jit(solution)/shard_map/ppermute | solution.py:10
  437.3 26.8 %collective-permute-start.22 = (f32[6,128,128]{2,1,0:T(8,128)S(1)}, f32[6,128,128]{2,1,0:T(8,128)S(1)}, u32[]{:S(2)}, u32[]{:S(2)}) collective-permute-start(f32[6,128,128]{2,1,0:T(8,128)S(1)} %get-tuple-element.75), channel_id=1, source_target_pairs={{16,0},{17,1},{18,2},{19,3},{20,4},{21,5},{22,6},{23,7},{24,8},{25... | collective-permute-start | bytes 1179656 | tf_op jit(solution)/shard_map/ppermute | solution.py:10
  445.8 18.2 %collective-permute-start.23 = (f32[6,128,128]{2,1,0:T(8,128)S(1)}, f32[6,128,128]{2,1,0:T(8,128)}, u32[]{:S(2)}, u32[]{:S(2)}) collective-permute-start(f32[6,128,128]{2,1,0:T(8,128)S(1)} %get-tuple-element.74), channel_id=1, source_target_pairs={{8,0},{9,1},{10,2},{11,3},{12,4},{13,5},{14,6},{15,7},{16,8},{17,9... | collective-permute-start | bytes 1179656 | tf_op jit(solution)/shard_map/ppermute | solution.py:10
  465.2 7.6 %collective-permute-start.24 = (f32[512,128]{1,0:T(8,128)S(1)}, f32[512,128]{1,0:T(8,128)S(1)}, u32[]{:S(2)}, u32[]{:S(2)}) collective-permute-start(f32[512,128]{1,0:T(8,128)S(1)} %fusion.42), channel_id=1, source_target_pairs={{0,1},{1,0},{2,3},{3,2},{4,5},{5,4},{6,7},{7,6},{8,9},{9,8},{10,11... | collective-permute-start | bytes 786440 | tf_op jit(solution)/shard_map/ppermute | solution.py:60
  472.8 13.8 %collective-permute-start.25 = (f32[512,128]{1,0:T(8,128)S(1)}, f32[512,128]{1,0:T(8,128)S(1)}, u32[]{:S(2)}, u32[]{:S(2)}) collective-permute-start(f32[512,128]{1,0:T(8,128)S(1)} %add_dynamic-update-slice_fusion), channel_id=1, source_target_pairs={{0,2},{1,3},{2,0},{3,1},{4,6},{5,7},{6,4},{7,5},{8,10},{9,11},{10,... | collective-permute-start | bytes 786440 | tf_op jit(solution)/shard_map/ppermute | solution.py:60
  486.6 15.3 %collective-permute-start.26 = (f32[512,128]{1,0:T(8,128)S(1)}, f32[512,128]{1,0:T(8,128)S(1)}, u32[]{:S(2)}, u32[]{:S(2)}) collective-permute-start(f32[512,128]{1,0:T(8,128)S(1)} %add.274), channel_id=1, source_target_pairs={{0,4},{1,5},{2,6},{3,7},{4,0},{5,1},{6,2},{7,3},{8,12},{9,13},{10,... | collective-permute-start | bytes 786440 | tf_op jit(solution)/shard_map/ppermute | solution.py:60
  502.0 5.3 collective-permute-start.27
  507.3 8.9 %collective-permute-start.28 = (f32[512,128]{1,0:T(8,128)S(1)}, f32[512,128]{1,0:T(8,128)S(1)}, u32[]{:S(2)}, u32[]{:S(2)}) collective-permute-start(f32[512,128]{1,0:T(8,128)S(1)} %add.276), channel_id=1, source_target_pairs={{0,16},{1,17},{2,18},{3,19},{4,20},{5,21},{6,22},{7,23},{8,24},{9,... | collective-permute-start | bytes 786440 | tf_op jit(solution)/shard_map/ppermute | solution.py:60
  586.9 11.8 %copy-start = (f32[512,128]{0,1:T(8,128)S(1)}, f32[512,128]{0,1:T(8,128)}, u32[]{:S(2)}) copy-start(f32[512,128]{0,1:T(8,128)} %all-reduce.5.cloned.1.call-done) | copy-start | bytes 786436
  586.9 11.7 %copy-start.1 = (f32[512,128]{0,1:T(8,128)S(1)}, f32[512,128]{0,1:T(8,128)}, u32[]{:S(2)}) copy-start(f32[512,128]{0,1:T(8,128)} %all-reduce.7.cloned.1.call-done) | copy-start | bytes 786436
  586.9 11.7 %copy-start.2 = (f32[512,128]{0,1:T(8,128)S(1)}, f32[512,128]{0,1:T(8,128)}, u32[]{:S(2)}) copy-start(f32[512,128]{0,1:T(8,128)} %all-reduce.9.cloned.1.call-done) | copy-start | bytes 786436
  586.9 11.7 %copy-start.3 = (f32[512,128]{0,1:T(8,128)S(1)}, f32[512,128]{0,1:T(8,128)}, u32[]{:S(2)}) copy-start(f32[512,128]{0,1:T(8,128)} %all-reduce.11.cloned.1.call-done) | copy-start | bytes 786436
  588.0 19.4 %collective-permute-start.29 = (f32[6,128,128]{2,1,0:T(8,128)}, f32[6,128,128]{2,1,0:T(8,128)}, u32[]{:S(2)}, u32[]{:S(2)}) collective-permute-start(f32[6,128,128]{2,1,0:T(8,128)} %get-tuple-element.70), channel_id=1, source_target_pairs={{24,0},{25,1},{26,2},{27,3},{28,4},{29,5},{30,6},{31,7},{0,8},{1,9... | collective-permute-start | bytes 1179656 | tf_op jit(solution)/shard_map/ppermute | solution.py:10
  589.2 27.6 %collective-permute-start.30 = (f32[6,128,128]{2,1,0:T(8,128)}, f32[6,128,128]{2,1,0:T(8,128)}, u32[]{:S(2)}, u32[]{:S(2)}) collective-permute-start(f32[6,128,128]{2,1,0:T(8,128)} %get-tuple-element.72), channel_id=1, source_target_pairs={{16,0},{17,1},{18,2},{19,3},{20,4},{21,5},{22,6},{23,7},{24,8},{25... | collective-permute-start | bytes 1179656 | tf_op jit(solution)/shard_map/ppermute | solution.py:10
  598.6 18.2 %collective-permute-start.31 = (f32[6,128,128]{2,1,0:T(8,128)}, f32[6,128,128]{2,1,0:T(8,128)}, u32[]{:S(2)}, u32[]{:S(2)}) collective-permute-start(f32[6,128,128]{2,1,0:T(8,128)} %get-tuple-element.71), channel_id=1, source_target_pairs={{8,0},{9,1},{10,2},{11,3},{12,4},{13,5},{14,6},{15,7},{16,8},{17,9... | collective-permute-start | bytes 1179656 | tf_op jit(solution)/shard_map/ppermute | solution.py:10
Sparse Core Ops, SparseCore 0:
  64.4 68.0 all-reduce.4
  217.1 66.7 all-reduce.6
  369.0 65.8 all-reduce.8
  519.6 67.0 all-reduce.10
